TPU v7x, 256 devices: a whole 4x4x8 slice. The times are simulated.
256 devices in a mesh: seq: 32 (over x, y, core), head: 8 (over z).
Axes of the slice: x: 4, y: 4, z: 8, core: 2. Of those that a mesh axis runs over, the one named last changes fastest.
Arguments:
- positions: int32 [16384], P('seq'), may hold values from 65535 to 98301, as said below
- queries: bfloat16 [16384, 32, 128], P('seq', 'head'), may hold values from -16 to 16
- keys: bfloat16 [16384, 16, 128], P('seq', 'head'), may hold values from -16 to 16
- values: bfloat16 [16384, 16, 128], P('seq', 'head'), may hold values from -6 to 6
- out_weight: bfloat16 [4096, 5376], P('head', 'seq'), may hold values from -0.1875 to 0.1875
- post_gain: float32 [5376], P('head'), may hold values from 0.25 to 1.75
- residual: bfloat16 [16384, 5376], P('seq', 'head'), may hold values from -6 to 6
Outputs:
- layer_out: bfloat16 [16384, 5376], P('seq', 'head')
Inputs may be any that keep to these rules, and one draw needn't show every extreme that they name: `positions`: strictly rising, by 1 or 2 from one token to the next; the last token's position is the most.
All inputs are finite; a program needn't handle non-finite values.
Results may differ from a plain program's by a relative error of at most 0.015.
Values may be sent and summed in bfloat16 or wider, within the bound.
No kernel may reach another device: no remote copies, remote signals or barrier semaphores. Data moves between devices by JAX's collectives and lax.ppermute only.
A program may use at most 64 MiB of HBM per device.

v0:
```python
import jax
import jax.numpy as jnp
from jax import lax
from jax.sharding import PartitionSpec as P

D = 5376
QUERY_HEADS = 32
KEY_VALUE_HEADS = 16
VISIBLE_SPAN = 1024
EPS = 1e-06
SCALE = 168.0 ** (-0.5)


def passed_along(value, axis, steps):
    count = lax.axis_size(axis)
    initial, last = (max(0, -steps), min(count, count - steps))
    return lax.ppermute(value, axis, [(source, source + steps) for source in range(initial, last)])


def copy_for_each(array, axis):
    length = lax.axis_size(axis)
    return lax.all_to_all(
        jnp.broadcast_to(array[None], (length, *array.shape)), axis, 0, 0, tiled=True
    )


def of_everyone(array, axis):
    return copy_for_each(array, axis).sum(axis=0)


def rotate(x, positions):
    half = x.shape[-1] // 2
    inverse = 10000.0 ** (-2.0 * jnp.arange(half, dtype=jnp.float32) / x.shape[-1])
    angle = positions.astype(jnp.float32)[:, None] * inverse[None, :]
    cosine = jnp.concatenate([jnp.cos(angle), jnp.cos(angle)], -1)[:, None, :]
    sine = jnp.concatenate([jnp.sin(angle), jnp.sin(angle)], -1)[:, None, :]
    source = x.astype(jnp.float32)
    turned = jnp.concatenate([-source[..., half:], source[..., :half]], -1)
    return (source * cosine + turned * sine).astype(jnp.bfloat16)


def on_device(positions, queries, keys, values, out_weight, post_gain, residual):
    rows = queries.shape[0]
    kv_heads = keys.shape[1]
    query_groups = QUERY_HEADS // KEY_VALUE_HEADS
    q_rot = rotate(queries, positions)
    stacked = jnp.stack([rotate(keys, positions), values], 0)
    reach = (VISIBLE_SPAN + rows - 2) // rows
    pieces = []
    carried = stacked
    for hop in range(reach):
        carried = passed_along(carried, "seq", 1)
        pieces.insert(0, carried)
    extended = jnp.concatenate(pieces + [stacked], axis=1)
    extra = extended.shape[1] - rows
    anchor = lax.axis_index("seq") * rows
    block_length = min(512, rows)
    query_tile_rows = q_rot.reshape(block_length, kv_heads, query_groups, -1)
    key_block = extended[0, 0 : extra + block_length]
    value_block = extended[1, 0 : extra + block_length]
    scores = (
        jnp.einsum("qhgd,khd->hgqk", query_tile_rows, key_block, preferred_element_type=jnp.float32)
        * SCALE
    )
    query_index = anchor + 0 + jnp.arange(block_length, dtype=jnp.int32)
    key_index = anchor - extra + 0 + jnp.arange(extra + block_length, dtype=jnp.int32)
    gap = query_index[:, None] - key_index[None, :]
    allowed = (gap >= 0) & (gap < VISIBLE_SPAN) & (key_index[None, :] >= 0)
    scores = jnp.where(allowed, scores, -1e30)
    top = jnp.max(scores, axis=-1, keepdims=True)
    weights = jnp.exp(scores - top)
    probs = (weights / jnp.sum(weights, axis=-1, keepdims=True)).astype(jnp.bfloat16)
    context = jnp.einsum("hgqk,khd->qhgd", probs, value_block, preferred_element_type=jnp.float32)
    outputs = context.astype(jnp.bfloat16).reshape(block_length, -1)
    context = outputs
    partial_value = jnp.dot(
        context,
        lax.all_gather(out_weight, "seq", axis=1, tiled=True),
        preferred_element_type=jnp.float32,
    )
    attended = lax.psum_scatter(
        partial_value.astype(jnp.bfloat16), "head", scatter_dimension=1, tiled=True
    ).astype(jnp.float32)
    squares = of_everyone(jnp.sum(attended * attended, axis=1), "head")
    scaled = attended * lax.rsqrt(squares / D + EPS)[:, None]
    result = residual.astype(jnp.float32) + post_gain[None, :] * scaled
    return result.astype(jnp.bfloat16)


def solution(mesh):
    return jax.shard_map(
        on_device,
        mesh=mesh,
        in_specs=(
            P("seq"),
            P("seq", "head", None),
            P("seq", "head", None),
            P("seq", "head", None),
            P("head", "seq"),
            P("head"),
            P("seq", "head"),
        ),
        out_specs=P("seq", "head"),
        check_vma=False,
    )
```

profile of v0, /device:TPU:2, one launch (start us, length us, event | category | flops | bytes accessed | tf_op | source)
XLA Modules:
  0.0 164.7 jit_solution(17591090239701363710)
XLA Ops:
  6.5 0.0 copy-start.3
  6.5 0.0 all-gather.2.cloned.1.call-start
  6.5 0.7 all-gather.2.cloned.1.call-update
  7.3 0.0 reduce-scatter.2.cloned.1.call-start
  7.3 0.7 convert_element_type.39
  8.0 1.0 copy.44
  9.0 1.0 multiply_cosine_fusion
  10.0 0.2 pad_maximum_fusion.1
  10.2 0.0 copy-start
  10.2 1.0 copy_convert_fusion
  11.3 0.2 slice_negate_fusion.1
  11.5 0.0 copy-done.3
  11.5 0.2 fusion.24
  11.7 0.0 copy-start.1
  11.7 0.9 pad_maximum_fusion
  12.6 1.9 %collective-permute-start = (bf16[2,512,2,128]{3,1,2,0:T(8,128)(2,1)}, bf16[2,512,2,128]{3,1,2,0:T(8,128)(2,1)}, u32[]{:S(2)}, u32[]{:S(2)}) collective-permute-start(bf16[2,512,2,128]{3,1,2,0:T(8,128)(2,1)} %pad_maximum_fusion), channel_id=1, source_target_pairs={{0,8},{8,16},{16,24},{24,32},{32,40},{40,48},{48,56},{56,64},{64,7... | collective-permute-start | bytes 1572872 | tf_op jit(solution)/shard_map/ppermute | solution.py:17
  14.5 0.0 copy-done.1
  14.5 0.0 copy-done
  14.5 0.1 convert_element_type.41
  14.6 0.1 slice.29
  14.8 0.0 copy-start.2
  14.8 0.6 slice_negate_fusion
  15.4 1.6 fusion.16
  17.1 0.0 copy-start.5
  17.1 8.4 %collective-permute-done = bf16[2,512,2,128]{3,1,2,0:T(8,128)(2,1)} collective-permute-done((bf16[2,512,2,128]{3,1,2,0:T(8,128)(2,1)}, bf16[2,512,2,128]{3,1,2,0:T(8,128)(2,1)}, u32[]{:S(2)}, u32[]{:S(2)}) %collective-permute-start) | collective-permute-done | bytes 524320 | tf_op jit(solution)/shard_map/ppermute | solution.py:17
  25.5 1.9 %collective-permute-start.1 = (bf16[2,512,2,128]{3,1,2,0:T(8,128)(2,1)}, bf16[2,512,2,128]{3,1,2,0:T(8,128)(2,1)S(1)}, u32[]{:S(2)}, u32[]{:S(2)}) collective-permute-start(bf16[2,512,2,128]{3,1,2,0:T(8,128)(2,1)} %collective-permute-done), channel_id=1, source_target_pairs={{0,8},{8,16},{16,24},{24,32},{32,40},{40,48},{48,56},{56,64},{64,7... | collective-permute-start | bytes 1572872 | tf_op jit(solution)/shard_map/ppermute | solution.py:17
  27.4 1.2 fusion.7
  28.6 11.5 %collective-permute-done.1 = bf16[2,512,2,128]{3,1,2,0:T(8,128)(2,1)S(1)} collective-permute-done((bf16[2,512,2,128]{3,1,2,0:T(8,128)(2,1)}, bf16[2,512,2,128]{3,1,2,0:T(8,128)(2,1)S(1)}, u32[]{:S(2)}, u32[]{:S(2)}) %collective-permute-start.1) | collective-permute-done | bytes 524320 | tf_op jit(solution)/shard_map/ppermute | solution.py:17
  40.1 0.0 copy-done.2
  40.1 1.2 maximum_maximum_fusion
  41.3 0.0 copy-done.5
  41.3 7.4 %fusion.27 = (f32[2,2,512]{2,1,0:T(2,128)S(1)}, f32[2,2,512,1536]{2,3,1,0:T(8,128)}) fusion(pred[512,1536]{0,1:T(8,128)(4,1)S(1)} %fusion.7, bf16[2,1536,2,128]{3,1,2,0:T(8,128)(2,1)S(1)} %maximum_maximum_fusion, bf16[512,2,2,128]{3,2,1,0:T(2,128)(2,1)S(1)} %bitcast.46), kind=kOutput, calls=%fused_computation.51 | convolution fusion | flops 817890816 | bytes 14688256 | tf_op jit(solution)/shard_map/sub | solution.py:71
  48.8 6.1 %fusion.14 = bf16[2,128,2,512]{3,1,2,0:T(8,128)(2,1)S(1)} fusion(f32[2,2,512,1536]{2,3,1,0:T(8,128)} %get-tuple-element.10, f32[2,2,512]{2,1,0:T(2,128)S(1)} %get-tuple-element.9, bf16[2,1536,2,128]{3,1,2,0:T(8,128)(2,1)S(1)} %maximum_maximum_fusion), kind=kOutput, calls=%fused_computation.22 | convolution fusion | flops 811859968 | bytes 13901824 | tf_op jit(solution)/shard_map/hgqk,khd->qhgd/dot_general | solution.py:73
  54.9 12.6 %all-gather.2.cloned.1.call-done = bf16[512,5376]{0,1:T(8,128)(2,1)} async-done(((bf16[512,168]{0,1:T(8,128)(2,1)}), bf16[512,5376]{0,1:T(8,128)(2,1)}) %all-gather.2.cloned.1.call-update) | async-done | bytes 5505040 | tf_op jit(solution)/shard_map/all_gather | solution.py:78
  67.4 7.3 %convolution_convert_fusion = bf16[512,5376]{0,1:T(8,128)(2,1)} fusion(bf16[512,5376]{0,1:T(8,128)(2,1)} %all-gather.2.cloned.1.call-done, bf16[512,512]{0,1:T(8,128)(2,1)S(1)} %bitcast.47), kind=kOutput, calls=%fused_computation.5 | convolution fusion | flops 2821324800 | bytes 11534336 | tf_op jit(solution)/shard_map/dot_general | solution.py:76
  74.7 0.0 copy-start.4
  74.7 0.0 copy-start.6
  74.7 0.0 reduce-scatter.2.cloned.1.call-update
  74.8 67.6 %reduce-scatter.2.cloned.1.call-done = bf16[512,672]{0,1:T(8,128)(2,1)} async-done(((bf16[512,5376]{0,1:T(8,128)(2,1)}), bf16[512,672]{0,1:T(8,128)(2,1)}) %reduce-scatter.2.cloned.1.call-update) | async-done | bytes 688144 | tf_op jit(solution)/shard_map/reduce_scatter | solution.py:81
  142.4 1.3 fusion.8
  143.7 11.9 %all_to_all.6 = f32[8,1,512]{2,1,0:T(1,128)S(1)} all-to-all(f32[8,1,512]{2,1,0:T(1,128)S(1)} %broadcast_in_dim.10), channel_id=1, replica_groups=mesh['seq'=32,'head'=8] {'head'}, dimensions={0} | all-to-all | bytes 32768 | tf_op jit(solution)/shard_map/all_to_all | solution.py:22
  155.6 0.0 copy-done.4
  155.7 0.0 copy-done.6
  155.7 2.2 %fusion.11 = bf16[512,672]{0,1:T(8,128)(2,1)} fusion(bf16[512,672]{0,1:T(8,128)(2,1)} %reduce-scatter.2.cloned.1.call-done, bf16[512,672]{0,1:T(8,128)(2,1)S(1)} %copy-done.4, f32[512]{0:T(512)S(1)} %add_rsqrt_fusion, f32[672]{0:T(1024)S(1)} %copy-done.6), kind=kLoop, calls=%fused_computation.20 | loop fusion | flops 2064384 | bytes 2069120 | tf_op jit(solution)/shard_map/convert_element_type | solution.py:87
  (7 shorter events, 0.1 us)
Async XLA Ops:
  6.5 4.9 %copy-start.3 = (bf16[512,2,128]{2,1,0:T(2,128)(2,1)S(1)}, bf16[512,2,128]{2,1,0:T(2,128)(2,1)}, u32[]{:S(2)}) copy-start(bf16[512,2,128]{2,1,0:T(2,128)(2,1)} %param.9) | copy-start | bytes 786436
  6.5 60.9 %all-gather.2.cloned.1.call-start = ((), (), s32[]{:S(2)}) async-start(), calls=%async_computation.2 | async-start | bytes 5677056 | tf_op jit(solution)/shard_map/all_gather | solution.py:78
  7.3 135.1 %reduce-scatter.2.cloned.1.call-start = ((), (), s32[]{:S(2)}) async-start(), calls=%async_computation.3 | async-start | bytes 6193152 | tf_op jit(solution)/shard_map/reduce_scatter | solution.py:81
  10.2 4.3 %copy-start = (bf16[512,4,128]{2,1,0:T(4,128)(2,1)S(1)}, bf16[512,4,128]{2,1,0:T(4,128)(2,1)}, u32[]{:S(2)}) copy-start(bf16[512,4,128]{2,1,0:T(4,128)(2,1)} %param.8) | copy-start | bytes 1572868
  11.7 2.8 %copy-start.1 = (bf16[1,512,2,128]{3,1,2,0:T(8,128)(2,1)}, bf16[1,512,2,128]{3,1,2,0:T(8,128)(2,1)S(1)}, u32[]{:S(2)}) copy-start(bf16[1,512,2,128]{3,1,2,0:T(8,128)(2,1)S(1)} %fusion.24) | copy-start | bytes 786436
  12.6 12.9 %collective-permute-start = (bf16[2,512,2,128]{3,1,2,0:T(8,128)(2,1)}, bf16[2,512,2,128]{3,1,2,0:T(8,128)(2,1)}, u32[]{:S(2)}, u32[]{:S(2)}) collective-permute-start(bf16[2,512,2,128]{3,1,2,0:T(8,128)(2,1)} %pad_maximum_fusion), channel_id=1, source_target_pairs={{0,8},{8,16},{16,24},{24,32},{32,40},{40,48},{48,56},{56,64},{64,7... | collective-permute-start | bytes 1572872 | tf_op jit(solution)/shard_map/ppermute | solution.py:17
  14.8 25.3 %copy-start.2 = (bf16[1,512,2,128]{3,1,2,0:T(8,128)(2,1)S(1)}, bf16[1,512,2,128]{3,1,2,0:T(8,128)(2,1)}, u32[]{:S(2)}) copy-start(bf16[1,512,2,128]{3,1,2,0:T(8,128)(2,1)} %copy-done.1) | copy-start | bytes 786436
  17.1 24.3 %copy-start.5 = (bf16[512,4,128]{2,1,0:T(4,128)(2,1)S(1)}, bf16[512,4,128]{2,1,0:T(4,128)(2,1)}, u32[]{:S(2)}) copy-start(bf16[512,4,128]{2,1,0:T(4,128)(2,1)} %fusion.16) | copy-start | bytes 1572868
  25.5 14.7 %collective-permute-start.1 = (bf16[2,512,2,128]{3,1,2,0:T(8,128)(2,1)}, bf16[2,512,2,128]{3,1,2,0:T(8,128)(2,1)S(1)}, u32[]{:S(2)}, u32[]{:S(2)}) collective-permute-start(bf16[2,512,2,128]{3,1,2,0:T(8,128)(2,1)} %collective-permute-done), channel_id=1, source_target_pairs={{0,8},{8,16},{16,24},{24,32},{32,40},{40,48},{48,56},{56,64},{64,7... | collective-permute-start | bytes 1572872 | tf_op jit(solution)/shard_map/ppermute | solution.py:17
  74.7 80.9 %copy-start.4 = (bf16[512,672]{0,1:T(8,128)(2,1)S(1)}, bf16[512,672]{0,1:T(8,128)(2,1)}, u32[]{:S(2)}) copy-start(bf16[512,672]{0,1:T(8,128)(2,1)} %param.13) | copy-start | bytes 2064388
  74.7 80.9 %copy-start.6 = (f32[672]{0:T(1024)S(1)}, f32[672]{0:T(1024)}, u32[]{:S(2)}) copy-start(f32[672]{0:T(1024)} %param.12) | copy-start | bytes 8068
Sparse Core Ops, SparseCore 0:
  9.9 57.4 all-gather.1
  74.9 67.4 reduce-scatter.1
where the time goes:
time: 165 us
  waiting for transfers between devices  101 us (61%)
  matrix products  20.9 us (13%)
  between operations  13.6 us (8%)
  other arithmetic  12.5 us (8%)
  blocking collectives  11.9 us (7%)
  starting transfers between devices  3.86 us (2%)
    reduce_scatter x1, waiting for transfers between devices, on_device(): lax.psum_scatter(partial_value.astype(jnp.bfloat16), 'head', scatter_dime...  67.6 us
    ppermute x2, waiting for transfers between devices, passed_along(): lax.ppermute(value, axis, [(source, source + steps) for source in range(i...  19.9 us
    all_gather x1, waiting for transfers between devices, on_device(): lax.all_gather(out_weight, 'seq', axis=1, tiled=True)  12.6 us
    all_to_all x1, blocking collectives, copy_for_each(): lax.all_to_all(jnp.broadcast_to(array[None], (length, *array.shape)), axi...  11.9 us
    sub x1, matrix products, on_device(): weights = jnp.exp(scores - top)  7.44 us
    dot_general x1, matrix products, on_device(): jnp.dot(context, lax.all_gather(out_weight, 'seq', axis=1, tiled=True), p...  7.32 us
    dot_general x1, matrix products, on_device(): jnp.einsum('hgqk,khd->qhgd', probs, value_block, preferred_element_type=j...  6.11 us
    ppermute x2, starting transfers between devices, passed_along(): lax.ppermute(value, axis, [(source, source + steps) for source in range(i...  3.82 us
  transfers between devices with their start and end apart: 4, of which 4 were waited for; matrix products, arithmetic and copies ran while one was open for 14% of the time, Pallas kernels for 0%

commit v1 on v0

--- a/solution.py
+++ b/solution.py
@@ -9,6 +9,12 @@
 VISIBLE_SPAN = 1024
 EPS = 1e-06
 SCALE = 168.0 ** (-0.5)
+
+
+def expand_table(raw, axis_id, d0):
+    response = lax.axis_size(axis_id)
+    newest = jnp.concatenate([raw] * response, axis=d0)
+    return lax.all_to_all(newest, axis_id, d0, d0, tiled=True)
 
 
 def passed_along(value, axis, steps):
@@ -74,9 +80,7 @@
     outputs = context.astype(jnp.bfloat16).reshape(block_length, -1)
     context = outputs
     partial_value = jnp.dot(
-        context,
-        lax.all_gather(out_weight, "seq", axis=1, tiled=True),
-        preferred_element_type=jnp.float32,
+        context, expand_table(out_weight, "seq", 1), preferred_element_type=jnp.float32
     )
     attended = lax.psum_scatter(
         partial_value.astype(jnp.bfloat16), "head", scatter_dimension=1, tiled=True

time: 165 us -> 230 us (1.39)
  waiting for transfers between devices: 101 us -> 144 us
  local copies, waits for them, and re-layouts: 1.14 us -> 17.8 us
  starting transfers between devices: 3.86 us -> 11.8 us
  other arithmetic: 12.5 us -> 10 us
    ppermute x2, waiting for transfers between devices: 19.9 us -> 76.1 us  [passed_along(): lax.ppermute(value, axis, [(source, source + steps) for source in range(i...]
    unnamed x15 -> x52, local copies, waits for them, and re-layouts: 1.01 us -> 17.7 us
    all_gather x1 -> x0, waiting for transfers between devices: 12.6 us -> none  [on_device(): lax.all_gather(out_weight, 'seq', axis=1, tiled=True)]
    all_to_all x0 -> x1, starting transfers between devices: none -> 7.8 us  [expand_table(): return lax.all_to_all(newest, axis_id, d0, d0, tiled=True)]
  transfers between devices with their start and end apart: 4 -> 4, of which waited for: 4 -> 3; matrix products, arithmetic and copies ran while one was open for 14% -> 9% of each run, Pallas kernels for 0% -> 0%
where the time goes in v1:
time: 230 us; the launch traced here: 229 us
  waiting for transfers between devices  144 us (63%)
  matrix products  20.4 us (9%)
  local copies, waits for them, and re-layouts  17.8 us (8%)
  between operations  13.8 us (6%)
  blocking collectives  11.9 us (5%)
  starting transfers between devices  11.8 us (5%)
  other arithmetic  10 us (4%)
    ppermute x2, waiting for transfers between devices, passed_along(): lax.ppermute(value, axis, [(source, source + steps) for source in range(i...  76.1 us
    reduce_scatter x1, waiting for transfers between devices, on_device(): lax.psum_scatter(partial_value.astype(jnp.bfloat16), 'head', scatter_dime...  67.4 us
    unnamed x52, local copies, waits for them, and re-layouts  17.7 us
    all_to_all x1, blocking collectives, copy_for_each(): lax.all_to_all(jnp.broadcast_to(array[None], (length, *array.shape)), axi...  11.9 us
    all_to_all x1, starting transfers between devices, expand_table(): return lax.all_to_all(newest, axis_id, d0, d0, tiled=True)  7.8 us
    sub x1, matrix products, on_device(): weights = jnp.exp(scores - top)  7.45 us
    dot_general x1, matrix products, on_device(): jnp.dot(context, expand_table(out_weight, 'seq', 1), preferred_element_ty...  7.33 us
    dot_general x1, matrix products, on_device(): jnp.einsum('hgqk,khd->qhgd', probs, value_block, preferred_element_type=j...  5.66 us
  transfers between devices with their start and end apart: 4, of which 3 were waited for; matrix products, arithmetic and copies ran while one was open for 9% of the time, Pallas kernels for 0%

profile of v1, /device:TPU:2, one launch (start us, length us, event | category | flops | bytes accessed | tf_op | source)
XLA Modules:
  0.0 229.3 jit_solution(11062172207799375831)
XLA Ops:
  6.5 0.0 copy-start
  6.5 1.0 constant_dynamic-update-slice_fusion.31
  7.5 0.9 constant_dynamic-update-slice_fusion.30
  8.5 0.9 constant_dynamic-update-slice_fusion.29
  9.4 0.9 constant_dynamic-update-slice_fusion.28
  10.3 0.9 constant_dynamic-update-slice_fusion.27
  11.3 0.9 constant_dynamic-update-slice_fusion.26
  12.2 0.9 constant_dynamic-update-slice_fusion.25
  13.2 0.9 constant_dynamic-update-slice_fusion.24
  14.1 0.9 constant_dynamic-update-slice_fusion.23
  15.0 0.9 constant_dynamic-update-slice_fusion.22
  16.0 0.9 constant_dynamic-update-slice_fusion.21
  16.9 0.9 constant_dynamic-update-slice_fusion.20
  17.8 0.9 constant_dynamic-update-slice_fusion.19
  18.8 0.9 constant_dynamic-update-slice_fusion.18
  19.7 0.9 constant_dynamic-update-slice_fusion.17
  20.6 0.9 constant_dynamic-update-slice_fusion.16
  21.6 0.0 copy-done
  21.9 0.0 copy-start.2
  21.9 2.4 %copy-done.2 = bf16[512,5376]{0,1:T(8,128)(2,1)} copy-done((bf16[512,5376]{0,1:T(8,128)(2,1)}, bf16[512,5376]{0,1:T(8,128)(2,1)S(1)}, u32[]{:S(2)}) %copy-start.2) | copy-done | bytes 5505048
  24.3 0.0 copy-start.9
  24.3 0.0 copy-start.7
  24.3 0.0 copy-start.5
  24.3 7.8 %all-to-all-start = ((bf16[512,32,168]{0,2,1:T(8,128)(2,1)}), bf16[512,32,168]{0,2,1:T(8,128)(2,1)}, u32[]{:S(2)}, u32[]{:S(2)}) async-start(bf16[512,32,168]{0,2,1:T(8,128)(2,1)} %bitcast.46), calls=%async_computation | async-start | bytes 11010048 | tf_op jit(solution)/shard_map/all_to_all | solution.py:17
  32.1 0.0 copy-start.1
  32.2 0.0 reduce-scatter.2.cloned.1.call-start
  32.2 0.0 copy-done.9
  32.2 1.0 multiply_cosine_fusion
  33.2 0.0 copy-done.7
  33.3 0.2 pad_maximum_fusion.1
  33.5 0.0 copy-done.5
  33.5 0.2 slice_negate_fusion.1
  33.8 0.2 fusion.24
  34.0 0.0 copy-start.3
  34.0 0.9 pad_maximum_fusion
  34.9 2.0 collective-permute-start
  36.9 0.0 copy-done.3
  36.9 0.0 copy-done.1
  36.9 0.1 convert_element_type.41
  37.1 0.1 slice.29
  37.2 0.0 copy-start.4
  37.2 0.6 slice_negate_fusion
  37.8 0.8 fusion.16
  38.7 66.5 %collective-permute-done = bf16[2,512,2,128]{3,1,2,0:T(8,128)(2,1)} collective-permute-done((bf16[2,512,2,128]{3,1,2,0:T(8,128)(2,1)}, bf16[2,512,2,128]{3,1,2,0:T(8,128)(2,1)}, u32[]{:S(2)}, u32[]{:S(2)}) %collective-permute-start) | collective-permute-done | bytes 524320 | tf_op jit(solution)/shard_map/ppermute | solution.py:23
  105.1 1.9 collective-permute-start.1
  107.1 1.2 fusion.7
  108.3 9.7 %collective-permute-done.1 = bf16[2,512,2,128]{3,1,2,0:T(8,128)(2,1)S(1)} collective-permute-done((bf16[2,512,2,128]{3,1,2,0:T(8,128)(2,1)}, bf16[2,512,2,128]{3,1,2,0:T(8,128)(2,1)S(1)}, u32[]{:S(2)}, u32[]{:S(2)}) %collective-permute-start.1) | collective-permute-done | bytes 524320 | tf_op jit(solution)/shard_map/ppermute | solution.py:23
  117.9 0.0 copy-done.4
  117.9 1.2 maximum_maximum_fusion
  119.1 7.4 %fusion.27 = (f32[2,2,512]{2,1,0:T(2,128)S(1)}, f32[2,2,512,1536]{2,3,1,0:T(8,128)}) fusion(pred[512,1536]{0,1:T(8,128)(4,1)S(1)} %fusion.7, bf16[2,1536,2,128]{3,1,2,0:T(8,128)(2,1)S(1)} %maximum_maximum_fusion, bf16[512,2,2,128]{3,2,1,0:T(2,128)(2,1)S(1)} %bitcast.49), kind=kOutput, calls=%fused_computation.83 | convolution fusion | flops 817890816 | bytes 14688256 | tf_op jit(solution)/shard_map/sub | solution.py:77
  126.5 5.7 %fusion.14 = bf16[2,128,2,512]{3,1,2,0:T(8,128)(2,1)S(1)} fusion(f32[2,2,512,1536]{2,3,1,0:T(8,128)} %get-tuple-element.10, f32[2,2,512]{2,1,0:T(2,128)S(1)} %get-tuple-element.9, bf16[2,1536,2,128]{3,1,2,0:T(8,128)(2,1)S(1)} %maximum_maximum_fusion), kind=kOutput, calls=%fused_computation.22 | convolution fusion | flops 811859968 | bytes 13901824 | tf_op jit(solution)/shard_map/hgqk,khd->qhgd/dot_general | solution.py:79
  132.2 0.0 all-to-all-done
  132.2 7.3 %convolution_convert_fusion = bf16[512,5376]{0,1:T(8,128)(2,1)} fusion(bf16[512,5376]{0,1:T(8,128)(2,1)} %bitcast.12, bf16[512,512]{0,1:T(8,128)(2,1)S(1)} %bitcast.50), kind=kOutput, calls=%fused_computation.5 | convolution fusion | flops 2821324800 | bytes 11534336 | tf_op jit(solution)/shard_map/dot_general | solution.py:82
  139.6 0.0 copy-start.6
  139.6 0.0 copy-start.8
  139.6 0.0 reduce-scatter.2.cloned.1.call-update
  139.6 67.4 %reduce-scatter.2.cloned.1.call-done = bf16[512,672]{0,1:T(8,128)(2,1)} async-done(((bf16[512,5376]{0,1:T(8,128)(2,1)}), bf16[512,672]{0,1:T(8,128)(2,1)}) %reduce-scatter.2.cloned.1.call-update) | async-done | bytes 688144 | tf_op jit(solution)/shard_map/reduce_scatter | solution.py:85
  207.0 1.3 fusion.8
  208.3 11.9 %all_to_all.18 = f32[8,1,512]{2,1,0:T(1,128)S(1)} all-to-all(f32[8,1,512]{2,1,0:T(1,128)S(1)} %broadcast_in_dim.10), channel_id=1, replica_groups=mesh['seq'=32,'head'=8] {'head'}, dimensions={0} | all-to-all | bytes 32768 | tf_op jit(solution)/shard_map/all_to_all | solution.py:28
  220.3 0.0 copy-done.6
  220.3 0.0 copy-done.8
  220.3 2.2 fusion.11
  (26 shorter events, 0.4 us)
Async XLA Ops:
  6.5 15.0 %copy-start = (bf16[512,168]{0,1:T(8,128)(2,1)S(1)}, bf16[512,168]{0,1:T(8,128)(2,1)}, u32[]{:S(2)}) copy-start(bf16[512,168]{0,1:T(8,128)(2,1)} %param.11) | copy-start | bytes 516100
  21.9 2.4 %copy-start.2 = (bf16[512,5376]{0,1:T(8,128)(2,1)}, bf16[512,5376]{0,1:T(8,128)(2,1)S(1)}, u32[]{:S(2)}) copy-start(bf16[512,5376]{0,1:T(8,128)(2,1)S(1)} %constant_dynamic-update-slice_fusion) | copy-start | bytes 16515076
  24.3 7.9 %copy-start.9 = (s32[512]{0:T(512)S(1)}, s32[512]{0:T(512)}, u32[]{:S(2)}) copy-start(s32[512]{0:T(512)} %param.7) | copy-start | bytes 6148
  24.3 8.9 %copy-start.7 = (bf16[512,2,128]{2,1,0:T(2,128)(2,1)S(1)}, bf16[512,2,128]{2,1,0:T(2,128)(2,1)}, u32[]{:S(2)}) copy-start(bf16[512,2,128]{2,1,0:T(2,128)(2,1)} %param.10) | copy-start | bytes 786436
  24.3 9.2 %copy-start.5 = (bf16[512,2,128]{2,1,0:T(2,128)(2,1)S(1)}, bf16[512,2,128]{2,1,0:T(2,128)(2,1)}, u32[]{:S(2)}) copy-start(bf16[512,2,128]{2,1,0:T(2,128)(2,1)} %param.9) | copy-start | bytes 786436
  24.3 107.9 %all-to-all-start = ((bf16[512,32,168]{0,2,1:T(8,128)(2,1)}), bf16[512,32,168]{0,2,1:T(8,128)(2,1)}, u32[]{:S(2)}, u32[]{:S(2)}) async-start(bf16[512,32,168]{0,2,1:T(8,128)(2,1)} %bitcast.46), calls=%async_computation | async-start | bytes 11010048 | tf_op jit(solution)/shard_map/all_to_all | solution.py:17
  32.1 4.8 %copy-start.1 = (bf16[512,4,128]{2,1,0:T(4,128)(2,1)S(1)}, bf16[512,4,128]{2,1,0:T(4,128)(2,1)}, u32[]{:S(2)}) copy-start(bf16[512,4,128]{2,1,0:T(4,128)(2,1)} %param.8) | copy-start | bytes 1572868
  32.2 174.8 %reduce-scatter.2.cloned.1.call-start = ((), (), s32[]{:S(2)}) async-start(), calls=%async_computation.3 | async-start | bytes 6193152 | tf_op jit(solution)/shard_map/reduce_scatter | solution.py:85
  34.0 2.9 %copy-start.3 = (bf16[1,512,2,128]{3,1,2,0:T(8,128)(2,1)}, bf16[1,512,2,128]{3,1,2,0:T(8,128)(2,1)S(1)}, u32[]{:S(2)}) copy-start(bf16[1,512,2,128]{3,1,2,0:T(8,128)(2,1)S(1)} %fusion.24) | copy-start | bytes 786436
  34.9 70.3 %collective-permute-start = (bf16[2,512,2,128]{3,1,2,0:T(8,128)(2,1)}, bf16[2,512,2,128]{3,1,2,0:T(8,128)(2,1)}, u32[]{:S(2)}, u32[]{:S(2)}) collective-permute-start(bf16[2,512,2,128]{3,1,2,0:T(8,128)(2,1)} %pad_maximum_fusion), channel_id=1, source_target_pairs={{0,8},{8,16},{16,24},{24,32},{32,40},{40,48},{48,56},{56,64},{64,7... | collective-permute-start | bytes 1572872 | tf_op jit(solution)/shard_map/ppermute | solution.py:23
  37.2 80.8 %copy-start.4 = (bf16[1,512,2,128]{3,1,2,0:T(8,128)(2,1)S(1)}, bf16[1,512,2,128]{3,1,2,0:T(8,128)(2,1)}, u32[]{:S(2)}) copy-start(bf16[1,512,2,128]{3,1,2,0:T(8,128)(2,1)} %copy-done.3) | copy-start | bytes 786436
  105.1 12.8 %collective-permute-start.1 = (bf16[2,512,2,128]{3,1,2,0:T(8,128)(2,1)}, bf16[2,512,2,128]{3,1,2,0:T(8,128)(2,1)S(1)}, u32[]{:S(2)}, u32[]{:S(2)}) collective-permute-start(bf16[2,512,2,128]{3,1,2,0:T(8,128)(2,1)} %collective-permute-done), channel_id=1, source_target_pairs={{0,8},{8,16},{16,24},{24,32},{32,40},{40,48},{48,56},{56,64},{64,7... | collective-permute-start | bytes 1572872 | tf_op jit(solution)/shard_map/ppermute | solution.py:23
  139.6 80.7 %copy-start.6 = (bf16[512,672]{0,1:T(8,128)(2,1)S(1)}, bf16[512,672]{0,1:T(8,128)(2,1)}, u32[]{:S(2)}) copy-start(bf16[512,672]{0,1:T(8,128)(2,1)} %param.13) | copy-start | bytes 2064388
  139.6 80.7 %copy-start.8 = (f32[672]{0:T(1024)S(1)}, f32[672]{0:T(1024)}, u32[]{:S(2)}) copy-start(f32[672]{0:T(1024)} %param.12) | copy-start | bytes 8068
Sparse Core Ops, SparseCore 0:
  139.7 67.2 reduce-scatter.1
